TPU v7x, 512 devices: a whole 4x8x8 slice. The times are simulated.
512 devices in a mesh: expert: 64 (over z, y), tensor: 8 (over x, core).
Axes of the slice: x: 4, y: 8, z: 8, core: 2. Of those that a mesh axis runs over, the one named last changes fastest.
Arguments:
- attn_out: bfloat16 [8192, 4096], P('expert', 'tensor'), may hold values from -6 to 6
- out_weight: bfloat16 [4096, 2048], P('tensor'), may hold values from -0.09375 to 0.09375
- residual: bfloat16 [8192, 2048], P(('expert', 'tensor')), may hold values from -6 to 6
- attn_gain: float32 [2048], replicated, may hold values from 0.1 to 1.9
- expert_ids: int32 [8192, 8], P('expert'), may hold values from 0 to 127, all different within a row; in each aligned block of 128 rows (0 to 127, 128 to 255, ...) at most 12 rows name the same one
- route_weights: float32 [8192, 8], P('expert'), may hold values from 0.05 to 0.3
- w_gate: bfloat16 [64, 2048, 1536], P('expert', None, 'tensor'), may hold values from -0.125 to 0.125
- w_up: bfloat16 [64, 2048, 1536], P('expert', None, 'tensor'), may hold values from -0.125 to 0.125
- w_down: bfloat16 [64, 1536, 2048], P('expert', 'tensor'), may hold values from -0.21875 to 0.21875
- input_gain: float32 [2048], replicated, may hold values from 0.1 to 1.9
- q_weight: bfloat16 [2048, 4096], P('expert', 'tensor'), may hold values from -0.125 to 0.125
- kv_weight: bfloat16 [2048, 1024], P('expert', 'tensor'), may hold values from -0.125 to 0.125
- q_gain: float32 [128], replicated, may hold values from 0.1 to 1.9
- k_gain: float32 [128], replicated, may hold values from 0.1 to 1.9
Outputs:
- next_residual: bfloat16 [8192, 2048], P(('expert', 'tensor'))
- queries: bfloat16 [8192, 4096], P('expert', 'tensor')
- keys_values: bfloat16 [8192, 1024], P('expert', 'tensor')
Inputs may be any that keep to these rules, and one draw needn't show every extreme that they name: `expert_ids`: each row names 8 different experts. In each aligned block of 128 rows no expert is named by more than 12 rows, and in some block one expert is named by exactly 12 rows.
All inputs are finite; a program needn't handle non-finite values.
Results may differ from a plain program's by a relative error of at most 0.012.
Values may be sent and summed in bfloat16 or wider, within the bound.
A program may use at most 64 MiB of HBM per device.

v0:
```python
import jax
import jax.numpy as jnp
from jax import lax
from jax.sharding import PartitionSpec as P

KV_HEADS = 4
TOP = 8
EPSILON = 1e-06


def normalize(values, gain):
    return values * lax.rsqrt(jnp.mean(values * values, axis=-1, keepdims=True) + EPSILON) * gain


def per_device(
    attn_out,
    out_weight,
    residual,
    attn_gain,
    expert_ids,
    route_weights,
    w_gate,
    w_up,
    w_down,
    input_gain,
    q_weight,
    kv_weight,
    q_gain,
    k_gain,
):
    n_expert = lax.axis_size("expert")
    n_tensor = lax.axis_size("tensor")
    share = n_tensor // 2
    tensor_index = lax.axis_index("tensor")
    group_rows = attn_out.shape[0]
    width = residual.shape[1]
    half = tensor_index // share
    capacity = 3 * group_rows * TOP // (4 * n_expert)
    all_experts = 2 * n_expert
    attn_rows = lax.psum_scatter(
        jnp.dot(attn_out, out_weight, preferred_element_type=jnp.float32),
        "tensor",
        scatter_dimension=0,
        tiled=True,
    )
    first_residual = (residual.astype(jnp.float32) + attn_rows).astype(jnp.bfloat16)
    normed = normalize(first_residual.astype(jnp.float32), attn_gain).astype(jnp.bfloat16)
    group_normed = lax.all_gather(normed, "tensor", axis=0, tiled=True)
    flat_ids = expert_ids.reshape(-1)
    onehot = (flat_ids[:, None] == jnp.arange(all_experts, dtype=jnp.int32)[None, :]).astype(
        jnp.int32
    )
    earlier = jnp.cumsum(onehot, axis=0) - onehot
    rank = jnp.sum(earlier * onehot, axis=1)
    dest = flat_ids * capacity + rank
    row_owner = jnp.arange(flat_ids.shape[0], dtype=jnp.int32) // TOP
    slot_row = jnp.full((all_experts * capacity,), group_rows, jnp.int32).at[dest].set(row_owner)
    slot_weight = (
        jnp.zeros((all_experts * capacity,), jnp.float32).at[dest].set(route_weights.reshape(-1))
    )
    own_slots = lax.dynamic_index_in_dim(
        slot_row.reshape(n_expert, 2, capacity), half, 1, keepdims=False
    )
    own_weights = lax.dynamic_index_in_dim(
        slot_weight.reshape(n_expert, 2, capacity), half, 1, keepdims=False
    )
    padded_rows = jnp.concatenate([group_normed, jnp.zeros((1, width), jnp.bfloat16)], axis=0)
    gate_w = w_gate[0]
    up_w = w_up[0]
    down_w = w_down[0]
    outgoing = jnp.take(padded_rows, own_slots, axis=0)
    arrived = lax.all_to_all(outgoing, "expert", split_axis=0, concat_axis=0, tiled=True)
    flat = arrived.reshape(-1, width)
    gate = jnp.dot(flat, gate_w, preferred_element_type=jnp.float32)
    up = jnp.dot(flat, up_w, preferred_element_type=jnp.float32)
    act = (jax.nn.silu(gate) * up).astype(jnp.bfloat16)
    part = jnp.dot(act, down_w, preferred_element_type=jnp.float32).astype(jnp.bfloat16)
    send_part = part.reshape(arrived.shape)
    returned = lax.all_to_all(send_part, "expert", split_axis=0, concat_axis=0, tiled=True)
    weighted = own_weights.reshape(-1)[:, None] * returned.reshape(-1, width).astype(jnp.float32)
    term = (
        jnp.zeros((group_rows + 1, width), jnp.float32)
        .at[own_slots.reshape(-1)]
        .add(weighted)[:group_rows]
    )
    expert_sum = lax.psum_scatter(
        term.astype(jnp.bfloat16), "tensor", scatter_dimension=0, tiled=True
    ).astype(jnp.float32)
    next_residual = (first_residual.astype(jnp.float32) + expert_sum).astype(jnp.bfloat16)
    own_normed = normalize(next_residual.astype(jnp.float32), input_gain).astype(jnp.bfloat16)
    next_normed = lax.all_gather(own_normed, "tensor", axis=0, tiled=True)
    query_cols = q_weight.shape[1]
    kv_cols = kv_weight.shape[1]
    query_raw = jnp.dot(
        next_normed,
        lax.all_gather(q_weight, "expert", axis=0, tiled=True),
        preferred_element_type=jnp.float32,
    )
    kv_raw = jnp.dot(
        next_normed,
        lax.all_gather(kv_weight, "expert", axis=0, tiled=True),
        preferred_element_type=jnp.float32,
    )
    head_size = q_gain.shape[0]
    queries = (
        normalize(query_raw.reshape(group_rows, -1, head_size), q_gain)
        .reshape(group_rows, query_cols)
        .astype(jnp.bfloat16)
    )
    heads_here = kv_cols // head_size
    head_number = tensor_index * heads_here + jnp.arange(heads_here, dtype=jnp.int32)
    is_key = head_number < KV_HEADS
    kv_shaped = kv_raw.reshape(group_rows, heads_here, head_size)
    keys_values = (
        jnp.where(is_key[None, :, None], normalize(kv_shaped, k_gain), kv_shaped)
        .reshape(group_rows, kv_cols)
        .astype(jnp.bfloat16)
    )
    return (next_residual, queries, keys_values)


def solution(mesh):
    return jax.shard_map(
        per_device,
        mesh=mesh,
        in_specs=(
            P("expert", "tensor"),
            P("tensor", None),
            P(("expert", "tensor"), None),
            P(),
            P("expert", None),
            P("expert", None),
            P("expert", None, "tensor"),
            P("expert", None, "tensor"),
            P("expert", "tensor", None),
            P(),
            P("expert", "tensor"),
            P("expert", "tensor"),
            P(),
            P(),
        ),
        out_specs=(P(("expert", "tensor"), None), P("expert", "tensor"), P("expert", "tensor")),
        check_vma=False,
    )
```

profile of v0, /device:TPU:2, one launch (start us, length us, event | category | flops | bytes accessed | tf_op | source)
XLA Modules:
  0.0 475.3 jit_solution(3789116620057749564)
XLA Ops:
  8.1 1.5 copy-done
  9.6 2.3 fusion.42
  12.0 0.1 copy.34
  12.3 0.1 copy.33
  12.4 0.1 mul.128
  12.5 0.1 copy.36
  12.6 0.2 fusion.17
  12.9 0.1 copy.37
  13.0 0.4 fusion.16
  13.4 4.3 scatter_custom_fusion
  17.7 0.1 reshape.200
  17.9 0.5 broadcast.190
  18.4 0.7 fusion.40
  19.3 32.0 %reduce-scatter.3.cloned.1.call-done = f32[16,2048]{1,0:T(8,128)} async-done(((f32[128,2048]{1,0:T(8,128)}), f32[16,2048]{1,0:T(8,128)}) %reduce-scatter.3.cloned.1.call-update) | async-done | bytes 131088 | tf_op jit(solution)/shard_map/reduce_scatter | solution.py:40
  51.3 1.0 fusion.26
  52.4 13.8 %all_gather.12 = bf16[128,2048]{1,0:T(8,128)(2,1)S(1)} all-gather(bf16[16,2048]{1,0:T(8,128)(2,1)S(1)} %fusion.28), channel_id=1, replica_groups=mesh['expert'=64,'tensor'=8] {'tensor'}, dimensions={0}, use_global_device_ids=true | all-gather | bytes 589824 | tf_op jit(solution)/shard_map/all_gather | solution.py:48
  66.3 4.3 gather_fusion
  70.6 6.1 %reshape.208 = bf16[64,12,2048]{2,1,0:T(8,128)(2,1)} reshape(bf16[768,2048]{1,0:T(8,128)(2,1)} %gather_fusion) | data formatting | bytes 6291456 | tf_op jit(solution)/shard_map/jit(_take)/gather | solution.py:71
  76.6 2.6 broadcast_select_fusion
  79.3 111.8 %all_to_all.10 = bf16[64,12,2048]{2,1,0:T(8,128)(2,1)} all-to-all(bf16[64,12,2048]{2,1,0:T(8,128)(2,1)S(1)} %broadcast_select_fusion), channel_id=1, replica_groups=mesh['expert'=64,'tensor'=8] {'expert'}, dimensions={0} | all-to-all | bytes 6291456 | tf_op jit(solution)/shard_map/all_to_all | solution.py:72
  191.1 6.2 %reshape.204 = bf16[768,2048]{1,0:T(8,128)(2,1)} reshape(bf16[64,12,2048]{2,1,0:T(8,128)(2,1)} %all_to_all.10) | data formatting | bytes 6291456 | tf_op jit(solution)/shard_map/reshape | solution.py:73
  197.3 3.3 fusion.7
  200.5 6.5 %convolution_convert_fusion = bf16[768,2048]{1,0:T(8,128)(2,1)} fusion(bf16[768,2048]{1,0:T(8,128)(2,1)} %reshape.204, bf16[1,192,2048]{2,1,0:T(8,128)(2,1)} %param.22, bf16[1,2048,192]{1,2,0:T(8,128)(2,1)} %param.21, f32[768,192]{0,1:T(8,128)S(1)} %fusion.7), kind=kOutput, calls=%fused_computation.7 | convolution fusion | flops 1210417152 | bytes 8454144 | tf_op jit(solution)/shard_map/dot_general | solution.py:77
  207.0 6.1 %reshape.205 = bf16[64,12,2048]{2,1,0:T(8,128)(2,1)} reshape(bf16[768,2048]{1,0:T(8,128)(2,1)} %convolution_convert_fusion) | data formatting | bytes 6291456 | tf_op jit(solution)/shard_map/reshape | solution.py:78
  213.1 12.7 %all-to-all-start.1 = ((bf16[64,12,2048]{2,1,0:T(8,128)(2,1)}), bf16[64,12,2048]{2,1,0:T(8,128)(2,1)}, u32[]{:S(2)}, u32[]{:S(2)}) async-start(bf16[64,12,2048]{2,1,0:T(8,128)(2,1)} %reshape.205), calls=%async_computation.2 | async-start | bytes 8388608 | tf_op jit(solution)/shard_map/all_to_all | solution.py:79
  225.9 0.1 reshape.201
  226.0 0.1 copy.38
  226.2 4.5 scatter_custom_fusion.1
  230.7 0.1 reshape.203
  230.9 0.1 dynamic-slice_reduce_fusion
  231.0 0.1 mul.130
  231.1 96.7 %all-to-all-done.1 = bf16[64,12,2048]{2,1,0:T(8,128)(2,1)} async-done(((bf16[64,12,2048]{2,1,0:T(8,128)(2,1)}), bf16[64,12,2048]{2,1,0:T(8,128)(2,1)}, u32[]{:S(2)}, u32[]{:S(2)}) %all-to-all-start.1) | async-done | bytes 3145760 | tf_op jit(solution)/shard_map/all_to_all | solution.py:79
  327.8 6.7 %reshape.206 = f32[768,2048]{1,0:T(8,128)} reshape(bf16[64,12,2048]{2,1,0:T(8,128)(2,1)} %all-to-all-done.1) | data formatting | bytes 9437184 | tf_op jit(solution)/shard_map/convert_element_type | solution.py:80
  334.5 15.8 %scatter_custom_fusion.2 = f32[129,2048]{1,0:T(8,128)S(1)} fusion(s32[768]{0:T(1024)S(1)} %fusion.37, f32[768,2048]{1,0:T(8,128)} %reshape.206, f32[768]{0:T(1024)S(1)} %mul.130, f32[]{:T(128)} %constant.76.clone.1), kind=kCustom, calls=%fused_computation.4 | custom fusion | flops 3145728 | bytes 7352324 | tf_op jit(solution)/shard_map/scatter-add | solution.py:84
  350.3 0.9 slice.20
  351.2 0.5 all-gather.2.cloned.1.call-update
  351.7 72.7 %all_gather.15 = bf16[2048,128]{1,0:T(8,128)(2,1)S(1)} all-gather(bf16[32,128]{1,0:T(8,128)(2,1)S(1)} %copy-done.4), channel_id=1, replica_groups=mesh['expert'=64,'tensor'=8] {'expert'}, dimensions={0}, use_global_device_ids=true | all-gather | bytes 532480 | tf_op jit(solution)/shard_map/all_gather | solution.py:101
  424.5 1.0 fusion.23
  425.6 13.1 %all_gather.13 = bf16[128,2048]{1,0:T(8,128)(2,1)S(1)} all-gather(bf16[16,2048]{1,0:T(8,128)(2,1)S(1)} %fusion.25), channel_id=1, replica_groups=mesh['expert'=64,'tensor'=8] {'tensor'}, dimensions={0}, use_global_device_ids=true | all-gather | bytes 589824 | tf_op jit(solution)/shard_map/all_gather | solution.py:91
  438.7 19.9 %all-gather.2.cloned.1.call-done = bf16[2048,512]{1,0:T(8,128)(2,1)} async-done(((bf16[32,512]{1,0:T(8,128)(2,1)}), bf16[2048,512]{1,0:T(8,128)(2,1)}) %all-gather.2.cloned.1.call-update) | async-done | bytes 2097168 | tf_op jit(solution)/shard_map/all_gather | solution.py:96
  458.6 2.8 fusion.41
  461.4 1.7 mul.146
  463.1 1.8 reduce_sum.51
  464.9 0.9 add_rsqrt_fusion
  465.7 0.4 multiply_reduce_fusion
  466.2 0.7 copy.41
  466.9 0.2 mul.147
  467.1 0.7 fusion.21
  (48 shorter events, 1.0 us)
Async XLA Ops:
  8.0 1.6 copy-start
  8.0 4.0 copy-start.3
  8.0 43.2 %reduce-scatter.3.cloned.1.call-start = ((), (), s32[]{:S(2)}) async-start(), calls=%async_computation.4 | async-start | bytes 1179648 | tf_op jit(solution)/shard_map/reduce_scatter | solution.py:40
  11.9 39.3 %copy-start.2 = (bf16[16,2048]{1,0:T(8,128)(2,1)S(1)}, bf16[16,2048]{1,0:T(8,128)(2,1)}, u32[]{:S(2)}) copy-start(bf16[16,2048]{1,0:T(8,128)(2,1)} %param.16) | copy-start | bytes 196612
  11.9 40.4 %copy-start.5 = (f32[2048]{0:T(1024)S(1)}, f32[2048]{0:T(1024)}, u32[]{:S(2)}) copy-start(f32[2048]{0:T(1024)} %param.17) | copy-start | bytes 24580
  213.1 12.9 %copy-start.7 = (f32[128,8]{0,1:T(8,128)S(1)}, f32[128,8]{0,1:T(8,128)}, u32[]{:S(2)}) copy-start(f32[128,8]{0,1:T(8,128)} %param.19) | copy-start | bytes 12292
  213.1 114.7 %all-to-all-start.1 = ((bf16[64,12,2048]{2,1,0:T(8,128)(2,1)}), bf16[64,12,2048]{2,1,0:T(8,128)(2,1)}, u32[]{:S(2)}, u32[]{:S(2)}) async-start(bf16[64,12,2048]{2,1,0:T(8,128)(2,1)} %reshape.205), calls=%async_computation.2 | async-start | bytes 8388608 | tf_op jit(solution)/shard_map/all_to_all | solution.py:79
  225.8 198.7 %reduce-scatter.5.cloned.1.call-start = ((), (), s32[]{:S(2)}) async-start(), calls=%async_computation.5 | async-start | bytes 589824 | tf_op jit(solution)/shard_map/reduce_scatter | solution.py:86
  334.5 17.3 %copy-start.4 = (bf16[32,128]{1,0:T(8,128)(2,1)S(1)}, bf16[32,128]{1,0:T(8,128)(2,1)}, u32[]{:S(2)}) copy-start(bf16[32,128]{1,0:T(8,128)(2,1)} %param.25) | copy-start | bytes 24580
  334.5 90.0 %copy-start.9 = (f32[128]{0:T(128)S(1)}, f32[128]{0:T(128)}, u32[]{:S(2)}) copy-start(f32[128]{0:T(128)} %param.26) | copy-start | bytes 1540
  334.5 91.0 %copy-start.6 = (f32[2048]{0:T(1024)S(1)}, f32[2048]{0:T(1024)}, u32[]{:S(2)}) copy-start(f32[2048]{0:T(1024)} %param.23) | copy-start | bytes 24580
  351.1 107.4 %all-gather.2.cloned.1.call-start = ((), (), s32[]{:S(2)}) async-start(), calls=%async_computation.6 | async-start | bytes 2129920 | tf_op jit(solution)/shard_map/all_gather | solution.py:96
  424.5 41.6 %copy-start.8 = (f32[128]{0:T(128)S(1)}, f32[128]{0:T(128)}, u32[]{:S(2)}) copy-start(f32[128]{0:T(128)} %param.27) | copy-start | bytes 1540
  425.5 41.6 %copy-start.1 = (bf16[16,2048]{1,0:T(8,128)(2,1)}, bf16[16,2048]{1,0:T(8,128)(2,1)S(1)}, u32[]{:S(2)}) copy-start(bf16[16,2048]{1,0:T(8,128)(2,1)S(1)} %get-tuple-element.16) | copy-start | bytes 196612
Sparse Core Ops, SparseCore 0:
  12.1 39.1 reduce-scatter.2
  351.3 53.9 reduce-scatter.4
Sparse Core Ops, SparseCore 1:
  354.7 103.8 all-gather.1
where the time goes:
time: 476 us; the launch traced here: 475 us
  blocking collectives  211 us (44%)
  waiting for transfers between devices  149 us (31%)
  local copies, waits for them, and re-layouts  46 us (10%)
  other arithmetic  24.7 us (5%)
  between operations  15.8 us (3%)
  matrix products  15.2 us (3%)
  starting transfers between devices  12.9 us (3%)
    all_to_all x1, blocking collectives, per_device(): lax.all_to_all(outgoing, 'expert', split_axis=0, concat_axis=0, tiled=True)  112 us
    all_to_all x1, waiting for transfers between devices, per_device(): lax.all_to_all(send_part, 'expert', split_axis=0, concat_axis=0, tiled=True)  96.7 us
    all_gather x1, blocking collectives, per_device(): lax.all_gather(kv_weight, 'expert', axis=0, tiled=True)  72.7 us
    reduce_scatter x1, waiting for transfers between devices, per_device(): lax.psum_scatter(jnp.dot(attn_out, out_weight, preferred_element_type=jnp...  32 us
    all_gather x1, waiting for transfers between devices, per_device(): lax.all_gather(q_weight, 'expert', axis=0, tiled=True)  19.9 us
    scatter-add x1, other arithmetic, per_device(): term = jnp.zeros((group_rows + 1, width), jnp.float32).at[own_slots.resha...  15.8 us
    all_gather x1, blocking collectives, per_device(): group_normed = lax.all_gather(normed, 'tensor', axis=0, tiled=True)  13.8 us
    all_gather x1, blocking collectives, per_device(): next_normed = lax.all_gather(own_normed, 'tensor', axis=0, tiled=True)  13.1 us
  transfers between devices with their start and end apart: 4, of which 3 were waited for; matrix products, arithmetic and copies ran while one was open for 3% of the time, Pallas kernels for 0%

commit v1 on v0

--- a/solution.py
+++ b/solution.py
@@ -6,6 +6,12 @@
 KV_HEADS = 4
 TOP = 8
 EPSILON = 1e-06
+
+
+def in_order(blocks, dim):
+    blocks = jnp.moveaxis(blocks, 0, dim)
+    lengths = blocks.shape
+    return blocks.reshape(*lengths[:dim], lengths[dim] * lengths[dim + 1], *lengths[dim + 2 :])
 
 
 def normalize(values, gain):
@@ -45,7 +51,19 @@
     )
     first_residual = (residual.astype(jnp.float32) + attn_rows).astype(jnp.bfloat16)
     normed = normalize(first_residual.astype(jnp.float32), attn_gain).astype(jnp.bfloat16)
-    group_normed = lax.all_gather(normed, "tensor", axis=0, tiled=True)
+    length = lax.axis_size("tensor")
+    pairs = [(i, (i + 1) % length) for i in range(length)]
+    back = [(b, a) for a, b in pairs]
+    lower, upper = ([], [])
+    for turn in range(length - 1):
+        if turn % 2 == 0:
+            lower.append(lax.ppermute(lower[-1] if lower else normed, "tensor", pairs))
+        else:
+            upper.append(lax.ppermute(upper[-1] if upper else normed, "tensor", back))
+    tiles = jnp.stack([*lower[::-1], normed, *upper])
+    shift = lax.axis_index("tensor") - len(lower)
+    tiles = tiles[(jnp.arange(length) - shift) % length]
+    group_normed = in_order(tiles, 0)
     flat_ids = expert_ids.reshape(-1)
     onehot = (flat_ids[:, None] == jnp.arange(all_experts, dtype=jnp.int32)[None, :]).astype(
         jnp.int32

time: 476 us -> 493 us (1.036)
  waiting for transfers between devices: 149 us -> 165 us
    all_gather x1, blocking collectives: 13.1 us -> 29.9 us  [per_device(): next_normed = lax.all_gather(own_normed, 'tensor', axis=0, tiled=True)]
    all_gather x1 -> x0, blocking collectives: 13.8 us -> none  [per_device(): group_normed = lax.all_gather(normed, 'tensor', axis=0, tiled=True)]
    ppermute x0 -> x7, waiting for transfers between devices: none -> 9.13 us  [the longest x4 9 us: per_device(): lower.append(lax.ppermute(lower[-1] if lower else normed, 'tensor', pairs))]
    ppermute x0 -> x7, starting transfers between devices: none -> 6.87 us  [the longest x3 6.85 us: per_device(): upper.append(lax.ppermute(upper[-1] if upper else normed, 'tensor', back))]
    all_gather x1, blocking collectives: 72.7 us -> 67.6 us  [per_device(): lax.all_gather(kv_weight, 'expert', axis=0, tiled=True)]
  transfers between devices with their start and end apart: 4 -> 11, of which waited for: 3 -> 9; matrix products, arithmetic and copies ran while one was open for 3% -> 3% of each run, Pallas kernels for 0% -> 0%
where the time goes in v1:
time: 493 us; the launch traced here: 492 us
  blocking collectives  207 us (42%)
  waiting for transfers between devices  165 us (33%)
  local copies, waits for them, and re-layouts  46.7 us (9%)
  other arithmetic  24.8 us (5%)
  starting transfers between devices  16.2 us (3%)
  matrix products  16 us (3%)
  between operations  15.9 us (3%)
    all_to_all x1, blocking collectives, per_device(): lax.all_to_all(outgoing, 'expert', split_axis=0, concat_axis=0, tiled=True)  110 us
    all_to_all x1, waiting for transfers between devices, per_device(): lax.all_to_all(send_part, 'expert', split_axis=0, concat_axis=0, tiled=True)  99.4 us
    all_gather x1, blocking collectives, per_device(): lax.all_gather(kv_weight, 'expert', axis=0, tiled=True)  67.6 us
    reduce_scatter x1, waiting for transfers between devices, per_device(): lax.psum_scatter(jnp.dot(attn_out, out_weight, preferred_element_type=jnp...  32.1 us
    all_gather x1, blocking collectives, per_device(): next_normed = lax.all_gather(own_normed, 'tensor', axis=0, tiled=True)  29.9 us
    all_gather x1, waiting for transfers between devices, per_device(): lax.all_gather(q_weight, 'expert', axis=0, tiled=True)  21.8 us
    scatter-add x1, other arithmetic, per_device(): term = jnp.zeros((group_rows + 1, width), jnp.float32).at[own_slots.resha...  15.8 us
    gather x2, local copies, waits for them, and re-layouts, per_device(): outgoing = jnp.take(padded_rows, own_slots, axis=0)  10.3 us
  transfers between devices with their start and end apart: 11, of which 9 were waited for; matrix products, arithmetic and copies ran while one was open for 3% of the time, Pallas kernels for 0%

profile of v1, /device:TPU:2, one launch (start us, length us, event | category | flops | bytes accessed | tf_op | source)
XLA Modules:
  0.0 492.1 jit_solution(10050082329031320825)
XLA Ops:
  8.1 1.5 copy-done
  9.6 2.3 fusion.44
  12.6 0.2 fusion.17
  13.0 0.4 fusion.16
  13.4 4.3 scatter_custom_fusion
  17.7 0.1 reshape.252
  17.9 0.5 broadcast.259
  18.4 0.7 fusion.42
  19.2 32.1 %reduce-scatter.3.cloned.1.call-done = f32[16,2048]{1,0:T(8,128)} async-done(((f32[128,2048]{1,0:T(8,128)}), f32[16,2048]{1,0:T(8,128)}) %reduce-scatter.3.cloned.1.call-update) | async-done | bytes 131088 | tf_op jit(solution)/shard_map/reduce_scatter | solution.py:46
  51.3 1.0 fusion.26
  52.6 3.6 collective-permute-done
  56.1 1.8 collective-permute-start.4
  57.9 1.9 collective-permute-done.1
  59.8 2.1 collective-permute-start.5
  61.9 1.8 collective-permute-done.2
  63.7 0.1 collective-permute-done.5
  63.8 3.0 collective-permute-start.6
  66.8 1.8 collective-permute-done.3
  68.8 0.6 gather_fusion
  69.4 4.3 gather_fusion.1
  73.7 6.1 %reshape.269 = bf16[64,12,2048]{2,1,0:T(8,128)(2,1)} reshape(bf16[768,2048]{1,0:T(8,128)(2,1)} %gather_fusion.1) | data formatting | bytes 6291456 | tf_op jit(solution)/shard_map/jit(_take)/gather | solution.py:89
  79.8 2.6 broadcast_select_fusion
  82.4 110.0 %all_to_all.10 = bf16[64,12,2048]{2,1,0:T(8,128)(2,1)} all-to-all(bf16[64,12,2048]{2,1,0:T(8,128)(2,1)S(1)} %broadcast_select_fusion), channel_id=1, replica_groups=mesh['expert'=64,'tensor'=8] {'expert'}, dimensions={0} | all-to-all | bytes 6291456 | tf_op jit(solution)/shard_map/all_to_all | solution.py:90
  192.4 6.2 %reshape.257 = bf16[768,2048]{1,0:T(8,128)(2,1)} reshape(bf16[64,12,2048]{2,1,0:T(8,128)(2,1)} %all_to_all.10) | data formatting | bytes 6291456 | tf_op jit(solution)/shard_map/reshape | solution.py:91
  198.6 3.9 fusion.7
  202.5 6.7 %convolution_convert_fusion = bf16[768,2048]{1,0:T(8,128)(2,1)} fusion(bf16[768,2048]{1,0:T(8,128)(2,1)} %reshape.257, bf16[1,192,2048]{2,1,0:T(8,128)(2,1)} %param.22, bf16[1,2048,192]{1,2,0:T(8,128)(2,1)} %param.21, f32[768,192]{0,1:T(8,128)} %fusion.7), kind=kOutput, calls=%fused_computation.8 | convolution fusion | flops 1210417152 | bytes 8454144 | tf_op jit(solution)/shard_map/dot_general | solution.py:95
  209.2 6.1 %reshape.258 = bf16[64,12,2048]{2,1,0:T(8,128)(2,1)} reshape(bf16[768,2048]{1,0:T(8,128)(2,1)} %convolution_convert_fusion) | data formatting | bytes 6291456 | tf_op jit(solution)/shard_map/reshape | solution.py:96
  215.2 9.2 %all-to-all-start.1 = ((bf16[64,12,2048]{2,1,0:T(8,128)(2,1)}), bf16[64,12,2048]{2,1,0:T(8,128)(2,1)}, u32[]{:S(2)}, u32[]{:S(2)}) async-start(bf16[64,12,2048]{2,1,0:T(8,128)(2,1)} %reshape.258), calls=%async_computation.2 | async-start | bytes 8388608 | tf_op jit(solution)/shard_map/all_to_all | solution.py:97
  224.8 4.5 scatter_custom_fusion.1
  229.3 0.1 reshape.255
  229.7 99.4 %all-to-all-done.1 = bf16[64,12,2048]{2,1,0:T(8,128)(2,1)} async-done(((bf16[64,12,2048]{2,1,0:T(8,128)(2,1)}), bf16[64,12,2048]{2,1,0:T(8,128)(2,1)}, u32[]{:S(2)}, u32[]{:S(2)}) %all-to-all-start.1) | async-done | bytes 3145760 | tf_op jit(solution)/shard_map/all_to_all | solution.py:97
  329.2 6.7 %reshape.259 = f32[768,2048]{1,0:T(8,128)} reshape(bf16[64,12,2048]{2,1,0:T(8,128)(2,1)} %all-to-all-done.1) | data formatting | bytes 9437184 | tf_op jit(solution)/shard_map/convert_element_type | solution.py:98
  335.8 15.8 %scatter_custom_fusion.2 = f32[129,2048]{1,0:T(8,128)S(1)} fusion(s32[768]{0:T(1024)S(1)} %fusion.37, f32[768,2048]{1,0:T(8,128)} %reshape.259, f32[768]{0:T(1024)S(1)} %mul.130, f32[]{:T(128)} %constant.90.clone.1), kind=kCustom, calls=%fused_computation.5 | custom fusion | flops 3145728 | bytes 7352324 | tf_op jit(solution)/shard_map/scatter-add | solution.py:102
  351.6 0.9 slice.22
  352.6 0.5 all-gather.2.cloned.1.call-update
  353.1 67.6 %all_gather.11 = bf16[2048,128]{1,0:T(8,128)(2,1)S(1)} all-gather(bf16[32,128]{1,0:T(8,128)(2,1)S(1)} %copy-done.5), channel_id=1, replica_groups=mesh['expert'=64,'tensor'=8] {'expert'}, dimensions={0}, use_global_device_ids=true | all-gather | bytes 532480 | tf_op jit(solution)/shard_map/all_gather | solution.py:119
  420.7 1.9 reduce-scatter.5.cloned.1.call-done
  422.6 1.0 fusion.23
  423.7 29.9 %all_gather.9 = bf16[128,2048]{1,0:T(8,128)(2,1)S(1)} all-gather(bf16[16,2048]{1,0:T(8,128)(2,1)S(1)} %fusion.25), channel_id=1, replica_groups=mesh['expert'=64,'tensor'=8] {'tensor'}, dimensions={0}, use_global_device_ids=true | all-gather | bytes 589824 | tf_op jit(solution)/shard_map/all_gather | solution.py:109
  453.6 21.8 %all-gather.2.cloned.1.call-done = bf16[2048,512]{1,0:T(8,128)(2,1)} async-done(((bf16[32,512]{1,0:T(8,128)(2,1)}), bf16[2048,512]{1,0:T(8,128)(2,1)}) %all-gather.2.cloned.1.call-update) | async-done | bytes 2097168 | tf_op jit(solution)/shard_map/all_gather | solution.py:114
  475.4 2.8 fusion.43
  478.2 1.7 mul.146
  479.9 1.8 reduce_sum.51
  481.7 0.9 add_rsqrt_fusion
  482.6 0.4 multiply_reduce_fusion
  483.0 0.7 copy.41
  483.8 0.2 mul.147
  484.0 0.7 fusion.21
  (74 shorter events, 2.1 us)
Async XLA Ops:
  8.0 1.6 copy-start
  8.0 4.0 copy-start.4
  8.0 43.2 %reduce-scatter.3.cloned.1.call-start = ((), (), s32[]{:S(2)}) async-start(), calls=%async_computation.4 | async-start | bytes 1179648 | tf_op jit(solution)/shard_map/reduce_scatter | solution.py:46
  11.9 39.3 %copy-start.2 = (bf16[16,2048]{1,0:T(8,128)(2,1)S(1)}, bf16[16,2048]{1,0:T(8,128)(2,1)}, u32[]{:S(2)}) copy-start(bf16[16,2048]{1,0:T(8,128)(2,1)} %param.16) | copy-start | bytes 196612
  11.9 40.4 %copy-start.3 = (f32[2048]{0:T(1024)S(1)}, f32[2048]{0:T(1024)}, u32[]{:S(2)}) copy-start(f32[2048]{0:T(1024)} %param.17) | copy-start | bytes 24580
  52.4 3.7 collective-permute-start
  56.1 3.7 collective-permute-start.1
  56.1 3.7 collective-permute-start.4
  59.8 3.9 collective-permute-start.2
  59.8 4.0 collective-permute-start.5
  63.7 4.9 collective-permute-start.3
  63.8 4.9 %collective-permute-start.6 = (bf16[16,2048]{1,0:T(8,128)(2,1)S(1)}, bf16[16,2048]{1,0:T(8,128)(2,1)S(1)}, u32[]{:S(2)}, u32[]{:S(2)}) collective-permute-start(bf16[16,2048]{1,0:T(8,128)(2,1)S(1)} %collective-permute-done.5), channel_id=1, source_target_pairs={{1,0},{2,1},{3,2},{4,3},{5,4},{6,5},{7,6},{0,7},{9,8},{10,9},{11,1... | collective-permute-start | bytes 196616 | tf_op jit(solution)/shard_map/ppermute | solution.py:62
  192.4 6.2 %copy-start.10 = (bf16[1,2048,192]{1,2,0:T(8,128)(2,1)S(1)}, bf16[1,2048,192]{1,2,0:T(8,128)(2,1)}, u32[]{:S(2)}) copy-start(bf16[1,2048,192]{1,2,0:T(8,128)(2,1)} %param.20) | copy-start | bytes 2359300
  215.2 9.4 %copy-start.7 = (f32[128,8]{0,1:T(8,128)S(1)}, f32[128,8]{0,1:T(8,128)}, u32[]{:S(2)}) copy-start(f32[128,8]{0,1:T(8,128)} %param.19) | copy-start | bytes 12292
  215.2 113.9 %all-to-all-start.1 = ((bf16[64,12,2048]{2,1,0:T(8,128)(2,1)}), bf16[64,12,2048]{2,1,0:T(8,128)(2,1)}, u32[]{:S(2)}, u32[]{:S(2)}) async-start(bf16[64,12,2048]{2,1,0:T(8,128)(2,1)} %reshape.258), calls=%async_computation.2 | async-start | bytes 8388608 | tf_op jit(solution)/shard_map/all_to_all | solution.py:97
  224.5 198.1 %reduce-scatter.5.cloned.1.call-start = ((), (), s32[]{:S(2)}) async-start(), calls=%async_computation.5 | async-start | bytes 589824 | tf_op jit(solution)/shard_map/reduce_scatter | solution.py:104
  335.8 17.3 %copy-start.5 = (bf16[32,128]{1,0:T(8,128)(2,1)S(1)}, bf16[32,128]{1,0:T(8,128)(2,1)}, u32[]{:S(2)}) copy-start(bf16[32,128]{1,0:T(8,128)(2,1)} %param.25) | copy-start | bytes 24580
  335.8 84.8 %copy-start.9 = (f32[128]{0:T(128)S(1)}, f32[128]{0:T(128)}, u32[]{:S(2)}) copy-start(f32[128]{0:T(128)} %param.26) | copy-start | bytes 1540
  335.8 87.8 %copy-start.6 = (f32[2048]{0:T(1024)S(1)}, f32[2048]{0:T(1024)}, u32[]{:S(2)}) copy-start(f32[2048]{0:T(1024)} %param.23) | copy-start | bytes 24580
  352.5 122.9 %all-gather.2.cloned.1.call-start = ((), (), s32[]{:S(2)}) async-start(), calls=%async_computation.6 | async-start | bytes 2129920 | tf_op jit(solution)/shard_map/all_gather | solution.py:114
  420.7 62.3 %copy-start.8 = (f32[128]{0:T(128)S(1)}, f32[128]{0:T(128)}, u32[]{:S(2)}) copy-start(f32[128]{0:T(128)} %param.27) | copy-start | bytes 1540
  423.6 60.3 %copy-start.1 = (bf16[16,2048]{1,0:T(8,128)(2,1)}, bf16[16,2048]{1,0:T(8,128)(2,1)S(1)}, u32[]{:S(2)}) copy-start(bf16[16,2048]{1,0:T(8,128)(2,1)S(1)} %get-tuple-element.16) | copy-start | bytes 196612
Sparse Core Ops, SparseCore 0:
  12.1 39.1 reduce-scatter.2
  352.6 69.9 reduce-scatter.4
Sparse Core Ops, SparseCore 1:
  356.1 119.3 all-gather.1
